TPU v7x, 256 devices: a whole 4x4x8 slice. The times are simulated.
256 devices in a mesh: seq: 8 (over z), ch: 32 (over x, y, core).
Axes of the slice: x: 4, y: 4, z: 8, core: 2. Of those that a mesh axis runs over, the one named last changes fastest.
Arguments:
- proj: bfloat16 [4, 2048, 3, 8192], P(None, ('seq', 'ch')), may hold values from -6 to 6
- short_w: float32 [3, 3, 8192], P(None, None, 'ch'), may hold values from -3.5 to 3.5
- long_filter: bfloat16 [512, 2048], P('ch'), may hold values from -1 to 1
Outputs:
- hyena_out: bfloat16 [4, 2048, 8192], P(None, ('seq', 'ch'))
All inputs are finite; a program needn't handle non-finite values.
Results may differ from a plain program's by a relative error of at most 0.0085.
Values may be sent and summed in bfloat16 or wider, within the bound.
A program may use at most 128 MiB of HBM per device.

v0:
```python
import jax
import jax.numpy as jnp
from jax import lax
from jax.experimental import pallas as pl
from jax.experimental.pallas import tpu as pltpu
from jax.sharding import PartitionSpec as P

MESH = pl.DeviceIdType.MESH
GSIZE = 16
LANES = 128
F32 = jnp.float32
BF16 = jnp.bfloat16


def kernel(nz, nc, proj, w_ref, lf_ref, out, kv, qb, qf, xs, xr, ys, yr, gs, toep, rev,
           kv_s, kv_r, q_s, q_r, h_s, h_r, x_s, x_r, y_s, y_r, o_s, o_r):
    z = lax.axis_index("seq")
    c = lax.axis_index("ch")
    seqs, _, rows, _ = proj.shape
    chans = kv.shape[-1]
    block = rows * nc
    halves = chans // LANES
    part = chans // nz
    per_half = LANES // part
    taps = w_ref.shape[0]
    chunk = 8
    chunks = nc // chunk
    span = chunk * rows

    def cols(p):
        return pl.ds(pl.multiple_of(p * chans, chans), chans)

    def settle(ref, sem):
        pltpu.make_async_copy(ref, ref, sem).wait()

    barrier = pltpu.get_barrier_semaphore()

    def greet_plane(k, carry):
        pl.semaphore_signal(barrier, inc=1, device_id=(z, lax.rem(c + k, nc)), device_id_type=MESH)
        return carry

    def greet_line(k, carry):
        pl.semaphore_signal(barrier, inc=1, device_id=(lax.rem(z + k, nz), c), device_id_type=MESH)
        return carry

    lax.fori_loop(1, nc, greet_plane, 0)
    lax.fori_loop(1, nz, greet_line, 0)
    own_kv = pltpu.make_async_copy(proj.at[:, 1:3, :, cols(c)], kv.at[c + 1], kv_r.at[c])
    own_kv.start()
    own_q = pltpu.make_async_copy(proj.at[:, 0, :, cols(c)], qb.at[c + 1], q_r.at[c])
    own_q.start()
    pl.semaphore_wait(barrier, nc - 1 + nz - 1)

    def send_kv(k, carry):
        p = lax.rem(c + k, nc)
        pltpu.make_async_remote_copy(
            src_ref=proj.at[:, 1:3, :, cols(p)], dst_ref=kv.at[c + 1], send_sem=kv_s,
            recv_sem=kv_r.at[c], device_id=(z, p), device_id_type=MESH).start()
        return carry

    def send_q(k, carry):
        p = lax.rem(c + k, nc)
        pltpu.make_async_remote_copy(
            src_ref=proj.at[:, 0, :, cols(p)], dst_ref=qb.at[c + 1], send_sem=q_s,
            recv_sem=q_r.at[c], device_id=(z, p), device_id_type=MESH).start()
        return carry

    lax.fori_loop(1, nc, send_kv, 0)
    lax.fori_loop(1, nc, send_q, 0)

    length = lf_ref.shape[1]
    pieces = length // LANES
    flip = (lax.broadcasted_iota(jnp.int32, (LANES, LANES), 0)
            + lax.broadcasted_iota(jnp.int32, (LANES, LANES), 1)) == LANES - 1
    flip = flip.astype(F32).astype(BF16)
    rev[:, 0:LANES] = jnp.zeros((lf_ref.shape[0], LANES), F32)
    for m in range(pieces):
        rev[:, (m + 1) * LANES:(m + 2) * LANES] = jnp.dot(
            lf_ref[:, m * LANES:(m + 1) * LANES], flip, preferred_element_type=F32)
    groups = part // GSIZE
    for g in range(groups):
        for m in range(pieces):
            pair = rev[pl.ds(z * groups + g, 1), m * LANES:(m + 2) * LANES]
            pair = jnp.broadcast_to(pair, (LANES, 2 * LANES))
            tile = pltpu.roll(pair, 1, 1, stride=1, stride_axis=0)[:, :LANES].astype(BF16)
            for th in range(2):
                for sh in range(2):
                    twice = m - th + sh
                    if twice % 2 == 0 and 0 <= twice // 2 < nz:
                        base = (twice // 2) * block + sh * LANES
                        toep[g, th * LANES:(th + 1) * LANES, base:base + LANES] = tile
        toep[g, 0:LANES, LANES:2 * LANES] = jnp.zeros((LANES, LANES), BF16)

    settle(kv.at[nc], kv_r.at[nc - 1])
    settle(qb.at[nc], q_r.at[nc - 1])

    @pl.when(z < nz - 1)
    def _():
        pltpu.make_async_remote_copy(
            src_ref=kv.at[nc], dst_ref=kv.at[0], send_sem=h_s.at[0], recv_sem=h_r.at[0],
            device_id=(z + 1, c), device_id_type=MESH).start()
        pltpu.make_async_remote_copy(
            src_ref=qb.at[nc], dst_ref=qb.at[0], send_sem=h_s.at[1], recv_sem=h_r.at[1],
            device_id=(z + 1, c), device_id_type=MESH).start()

    @pl.when(z == 0)
    def _():
        kv[0] = jnp.zeros(kv.shape[1:], BF16)
        qb[0] = jnp.zeros(qb.shape[1:], BF16)

    def feature(ext, i, h):
        total = None
        for k in range(taps):
            term = w_ref[k, i:i + 1, h * LANES:(h + 1) * LANES] * ext[rows - k:rows - k + span]
            total = term if total is None else total + term
        return total

    def product_chunk(k, carry):
        j = lax.rem(k + 1, chunks)
        s0 = j * chunk

        def arrive(s, carry):
            settle(kv.at[s + 1], kv_r.at[s])
            return carry

        first = s0 - (k == 0).astype(jnp.int32)
        last = s0 + chunk - (k >= chunks - 2).astype(jnp.int32)
        lax.fori_loop(first, last, arrive, 0)

        @pl.when(jnp.logical_and(j == 0, z > 0))
        def _():
            settle(kv.at[0], h_r.at[0])

        t0 = pl.multiple_of(j * span, span)
        for h in range(halves):
            prods = []
            for n in range(seqs):
                feats = []
                for i in range(2):
                    ext = kv[pl.ds(s0, chunk + 1), n, i, :, h * LANES:(h + 1) * LANES].astype(F32)
                    feats.append(feature(ext.reshape((chunk + 1) * rows, LANES), i + 1, h))
                prods.append(feats[0] * feats[1])
            for k in range(per_half):
                tile = jnp.concatenate([p[:, k * part:(k + 1) * part] for p in prods], axis=1)
                xs[h * per_half + k, pl.ds(t0, span), :] = tile.astype(BF16)
        return carry

    lax.fori_loop(0, chunks, product_chunk, 0)

    def send_x(k, carry):
        p = lax.rem(z + k, nz)
        pltpu.make_async_remote_copy(
            src_ref=xs.at[p], dst_ref=xr.at[nz - 1 - z], send_sem=x_s, recv_sem=x_r.at[z],
            device_id=(p, c), device_id_type=MESH).start()
        return carry

    lax.fori_loop(1, nz, send_x, 0)
    pltpu.make_async_copy(xs.at[z], xr.at[nz - 1 - z], x_r.at[z]).start()
    xr[nz] = jnp.zeros(xr.shape[1:], BF16)

    def query_chunk(k, carry):
        j = lax.rem(k + 1, chunks)
        s0 = j * chunk

        def arrive(s, carry):
            settle(qb.at[s + 1], q_r.at[s])
            return carry

        first = s0 - (k == 0).astype(jnp.int32)
        last = s0 + chunk - (k >= chunks - 2).astype(jnp.int32)
        lax.fori_loop(first, last, arrive, 0)

        @pl.when(jnp.logical_and(j == 0, z > 0))
        def _():
            settle(qb.at[0], h_r.at[1])

        for h in range(halves):
            for n in range(seqs):
                ext = qb[pl.ds(s0, chunk + 1), n, :, h * LANES:(h + 1) * LANES].astype(F32)
                value = feature(ext.reshape((chunk + 1) * rows, LANES), 0, h)
                qf[pl.ds(s0, chunk), n, :, h * LANES:(h + 1) * LANES] = value.astype(BF16).reshape(
                    chunk, rows, LANES)
        return carry

    lax.fori_loop(0, chunks, query_chunk, 0)

    for s in range(nz):
        settle(xr.at[nz - 1 - s], x_r.at[s])
    lane = lax.broadcasted_iota(jnp.int32, (1, 2 * LANES), 1)
    for m in range(nz // 2):
        lags = 2 * m + 2
        even = xr[nz - 1 - 2 * m:nz - 1 - 2 * m + lags].reshape(lags * block, LANES)
        odd = xr[nz - 2 - 2 * m:nz - 2 - 2 * m + lags].reshape(lags * block, LANES)
        both = jnp.concatenate([even, odd], axis=1)
        total = None
        for g in range(groups):
            keep = ((lane // GSIZE) % groups == g).astype(F32).astype(BF16)
            term = jnp.dot(toep[g, :, 0:lags * block], both * keep, preferred_element_type=F32)
            total = term if total is None else total + term
        ys[2 * m] = total[:, :LANES].astype(BF16)
        ys[2 * m + 1] = total[:, LANES:].astype(BF16)

    def send_y(k, carry):
        p = lax.rem(z + k, nz)
        pltpu.make_async_remote_copy(
            src_ref=ys.at[p], dst_ref=yr.at[z], send_sem=y_s, recv_sem=y_r.at[z],
            device_id=(p, c), device_id_type=MESH).start()
        return carry

    lax.fori_loop(1, nz, send_y, 0)
    pltpu.make_async_copy(ys.at[z], yr.at[z], y_r.at[z]).start()
    for s in range(nz):
        settle(yr.at[s], y_r.at[s])

    def gate_chunk(j, carry):
        s0 = j * chunk
        t0 = pl.multiple_of(j * span, span)
        for h in range(halves):
            tiles = [yr[h * per_half + k, pl.ds(t0, span), :].astype(F32) for k in range(per_half)]
            for n in range(seqs):
                filtered = jnp.concatenate([t[:, n * part:(n + 1) * part] for t in tiles], axis=1)
                query = qf[pl.ds(s0, chunk), n, :, h * LANES:(h + 1) * LANES].astype(F32)
                gated = query * filtered.reshape(chunk, rows, LANES)
                gs[pl.ds(s0, chunk), n, :, h * LANES:(h + 1) * LANES] = gated.astype(BF16)

        def send_out(s, carry):
            @pl.when(s != c)
            def _():
                pltpu.make_async_remote_copy(
                    src_ref=gs.at[s], dst_ref=out.at[:, :, cols(c)], send_sem=o_s, recv_sem=o_r.at[c],
                    device_id=(z, s), device_id_type=MESH).start()

            @pl.when(s == c)
            def _():
                pltpu.make_async_copy(gs.at[c], out.at[:, :, cols(c)], o_r.at[c]).start()
            return carry

        lax.fori_loop(s0, s0 + chunk, send_out, 0)
        return carry

    lax.fori_loop(0, chunks, gate_chunk, 0)

    def landed(s, carry):
        settle(out.at[:, :, cols(s)], o_r.at[s])
        return carry

    lax.fori_loop(0, nc, landed, 0)
    settle(kv.at[1:nc], kv_s)
    settle(qb.at[1:nc], q_s)
    settle(xs.at[1:nz], x_s)
    settle(ys.at[1:nz], y_s)
    settle(gs.at[1:nc], o_s)

    @pl.when(z < nz - 1)
    def _():
        settle(kv.at[nc], h_s.at[0])
        settle(qb.at[nc], h_s.at[1])


def solution(mesh):
    nz, nc = mesh.shape["seq"], mesh.shape["ch"]

    def shards(proj, short_w, long_filter):
        seqs, rows, _, width = proj.shape
        chans = width // nc
        block = rows * nc
        groups, length = long_filter.shape
        own = chans // nz // GSIZE
        by_component = jnp.transpose(proj, (0, 2, 1, 3))
        dma = pltpu.SemaphoreType.DMA
        return pl.pallas_call(
            lambda *refs: kernel(nz, nc, *refs),
            out_shape=jax.ShapeDtypeStruct((seqs, rows, width), BF16),
            in_specs=[
                pl.BlockSpec(memory_space=pl.ANY),
                pl.BlockSpec(memory_space=pltpu.VMEM),
                pl.BlockSpec(memory_space=pltpu.VMEM),
            ],
            out_specs=pl.BlockSpec(memory_space=pl.ANY),
            scratch_shapes=[
                pltpu.VMEM((nc + 1, seqs, 2, rows, chans), BF16),
                pltpu.VMEM((nc + 1, seqs, rows, chans), BF16),
                pltpu.VMEM((nc, seqs, rows, chans), BF16),
                pltpu.VMEM((nz, block, LANES), BF16),
                pltpu.VMEM((nz + 1, block, LANES), BF16),
                pltpu.VMEM((nz, block, LANES), BF16),
                pltpu.VMEM((nz, block, LANES), BF16),
                pltpu.VMEM((nc, seqs, rows, chans), BF16),
                pltpu.VMEM((own, block, length), BF16),
                pltpu.VMEM((groups, length + LANES), F32),
                dma, dma((nc,)), dma, dma((nc,)), dma((2,)), dma((2,)),
                dma, dma((nz,)), dma, dma((nz,)), dma, dma((nc,)),
            ],
            compiler_params=pltpu.CompilerParams(collective_id=0, has_side_effects=True),
            name="hyena",
        )(by_component, short_w, long_filter)

    in_specs = (P(None, ("seq", "ch"), None, None), P(None, None, "ch"), P("ch", None))
    out_specs = P(None, ("seq", "ch"), None)
    return jax.shard_map(shards, mesh=mesh, in_specs=in_specs, out_specs=out_specs, check_vma=False)
```

profile of v0, /device:TPU:1, one launch (start us, length us, event | category | flops | bytes accessed | tf_op | source)
XLA Modules:
  0.0 71.6 jit_solution(8364820279261495149)
XLA Ops:
  0.0 69.8 %hyena.1 = bf16[4,8,8192]{2,1,0:T(8,128)(2,1)} custom-call(bf16[4,3,8,8192]{3,2,1,0:T(8,128)(2,1)} %bitcast.1, f32[3,3,256]{2,1,0:T(4,128)} %refs_1_.1, bf16[16,2048]{1,0:T(8,128)(2,1)} %refs_2_.1), custom_call_target="tpu_custom_call" | custom-call | tf_op jit(solution)/shard_map/hyena/pallas_call | solution.py:271
  69.8 1.9 %copy.5 = bf16[4,8,8192]{2,1,0:T(8,128)(2,1)} copy(bf16[4,8,8192]{2,1,0:T(8,128)(2,1)} %hyena.1) | data formatting | bytes 1048576
where the time goes:
time: 71.9 us; the launch traced here: 71.6 us
  Pallas kernels  69.8 us (97%)
  local copies, waits for them, and re-layouts  1.87 us (3%)
    pallas_call x1, Pallas kernels, shards(): pl.pallas_call(lambda *refs: kernel(nz, nc, *refs), out_shape=jax.ShapeDt...  69.8 us
    unnamed x1, local copies, waits for them, and re-layouts  1.87 us

commit v1 on v0

v1 whole, which is shorter than its diff:
```python
import jax
import jax.numpy as jnp
from jax import lax
from jax.experimental import pallas as pl
from jax.experimental.pallas import tpu as pltpu
from jax.sharding import PartitionSpec as P

MESH = pl.DeviceIdType.MESH
GSIZE = 16
LANES = 128
F32 = jnp.float32
BF16 = jnp.bfloat16


def kernel(nz, nc, proj, w_ref, lf_ref, out, kv, qb, qf, xs, xr, ys, yr, gs, toep, rev,
           kv_s, kv_r, q_s, q_r, h_s, h_r, x_s, x_r, y_s, y_r, o_s, o_r):
    z = lax.axis_index("seq")
    c = lax.axis_index("ch")
    seqs, _, rows, _ = proj.shape
    halves, chans = kv.shape[0], qb.shape[-1]
    block = rows * nc
    part = chans // nz
    per_half = LANES // part
    taps = w_ref.shape[0]
    chunk = 8
    chunks = nc // chunk
    span = chunk * rows
    own_half = lax.rem(z, halves)
    side = 4
    around = (0, 2, 1, 3)

    def cols(p):
        return pl.ds(pl.multiple_of(p * chans, chans), chans)

    def half_cols(p, h):
        return pl.ds(pl.multiple_of(p * chans + h * LANES, LANES), LANES)

    def settle(ref, sem):
        pltpu.make_async_copy(ref, ref, sem).wait()

    def partner(k):
        x = lax.rem(c // 8 + 2 + k // 8, side)
        y = lax.rem(c // 2 + 2 + k // 2, side)
        return x * 8 + y * 2 + lax.rem(c + k, 2)

    def each_partner(body):
        def step(k, carry):
            body(partner(k))
            return carry

        lax.fori_loop(0, 20, step, 0)
        lax.fori_loop(21, nc, step, 0)

    barrier = pltpu.get_barrier_semaphore()

    def greet(p):
        pl.semaphore_signal(barrier, inc=1, device_id=(z, p), device_id_type=MESH)

    def greet_line(k, carry):
        pl.semaphore_signal(barrier, inc=1, device_id=(lax.rem(z + k, nz), c), device_id_type=MESH)
        return carry

    each_partner(greet)
    lax.fori_loop(1, nz, greet_line, 0)
    for h in range(halves):
        pltpu.make_async_copy(
            proj.at[:, 1:3, :, half_cols(c, h)], kv.at[h, c + 1], kv_r.at[h, c]).start()
    pltpu.make_async_copy(proj.at[:, 0, :, cols(c)], qb.at[c + 1], q_r).start()
    pl.semaphore_wait(barrier, nc - 1 + nz - 1)

    for h in range(halves):
        def send_kv(p, h=h):
            pltpu.make_async_remote_copy(
                src_ref=proj.at[:, 1:3, :, half_cols(p, h)], dst_ref=kv.at[h, c + 1], send_sem=kv_s,
                recv_sem=kv_r.at[h, c], device_id=(z, p), device_id_type=MESH).start()

        each_partner(send_kv)

    length = lf_ref.shape[1]
    pieces = length // LANES
    flip = (lax.broadcasted_iota(jnp.int32, (LANES, LANES), 0)
            + lax.broadcasted_iota(jnp.int32, (LANES, LANES), 1)) == LANES - 1
    flip = flip.astype(F32).astype(BF16)
    rev[:, 0:LANES] = jnp.zeros((lf_ref.shape[0], LANES), F32)
    for m in range(pieces):
        rev[:, (m + 1) * LANES:(m + 2) * LANES] = jnp.dot(
            lf_ref[:, m * LANES:(m + 1) * LANES], flip, preferred_element_type=F32)
    groups = part // GSIZE
    own_row = (own_half * LANES + (z // halves) * part) // GSIZE
    for g in range(groups):
        for m in range(pieces):
            pair = rev[pl.ds(own_row + g, 1), m * LANES:(m + 2) * LANES]
            pair = jnp.broadcast_to(pair, (LANES, 2 * LANES))
            tile = pltpu.roll(pair, 1, 1, stride=1, stride_axis=0)[:, :LANES].astype(BF16)
            for th in range(2):
                for sh in range(2):
                    twice = m - th + sh
                    if twice % 2 == 0 and 0 <= twice // 2 < nz:
                        base = (twice // 2) * block + sh * LANES
                        toep[g, th * LANES:(th + 1) * LANES, base:base + LANES] = tile
        toep[g, 0:LANES, LANES:2 * LANES] = jnp.zeros((LANES, LANES), BF16)

    xr[nz] = jnp.zeros(xr.shape[1:], BF16)

    @pl.when(z == 0)
    def _():
        for h in range(halves):
            kv[h, 0] = jnp.zeros(kv.shape[2:], BF16)
        qb[0] = jnp.zeros(qb.shape[1:], BF16)

    def feature(ext, i, h):
        total = None
        for k in range(taps):
            term = w_ref[k, i:i + 1, h * LANES:(h + 1) * LANES] * ext[rows - k:rows - k + span]
            total = term if total is None else total + term
        return total

    for h in range(halves):
        settle(kv.at[h, nc], kv_r.at[h, nc - 1])

        @pl.when(z < nz - 1)
        def _():
            pltpu.make_async_remote_copy(
                src_ref=kv.at[h, nc], dst_ref=kv.at[h, 0], send_sem=h_s.at[h], recv_sem=h_r.at[h],
                device_id=(z + 1, c), device_id_type=MESH).start()

        def product_chunk(k, carry, h=h):
            j = lax.rem(k + 1, chunks)
            s0 = j * chunk

            def arrive(s, carry):
                settle(kv.at[h, s + 1], kv_r.at[h, s])
                return carry

            first = s0 - (k == 0).astype(jnp.int32)
            last = s0 + chunk - (k >= chunks - 2).astype(jnp.int32)
            lax.fori_loop(first, last, arrive, 0)

            @pl.when(jnp.logical_and(j == 0, z > 0))
            def _():
                settle(kv.at[h, 0], h_r.at[h])

            t0 = pl.multiple_of(j * span, span)
            prods = []
            for n in range(seqs):
                feats = []
                for i in range(2):
                    ext = kv[h, pl.ds(s0, chunk + 1), n, i].astype(F32)
                    feats.append(feature(ext.reshape((chunk + 1) * rows, LANES), i + 1, h))
                prods.append(feats[0] * feats[1])
            for k in range(per_half):
                tile = jnp.concatenate([p[:, k * part:(k + 1) * part] for p in prods], axis=1)
                xs[halves * k + h, pl.ds(t0, span), :] = tile.astype(BF16)
            return carry

        lax.fori_loop(0, chunks, product_chunk, 0)

        for a in (2, 1, 3, 0):
            p = halves * lax.rem(z // halves + a, per_half) + h

            def send_x(p=p):
                pltpu.make_async_remote_copy(
                    src_ref=xs.at[p], dst_ref=xr.at[nz - 1 - z], send_sem=x_s, recv_sem=x_r.at[z],
                    device_id=(p, c), device_id_type=MESH).start()

            if a > 0:
                send_x()
            else:
                pl.when(own_half != h)(send_x)

        @pl.when(own_half == h)
        def _():
            pltpu.make_async_copy(xs.at[z], xr.at[nz - 1 - z], x_r.at[z]).start()

        if h == 0:
            def send_q(p):
                pltpu.make_async_remote_copy(
                    src_ref=proj.at[:, 0, :, cols(p)], dst_ref=qb.at[c + 1], send_sem=q_s,
                    recv_sem=q_r, device_id=(z, p), device_id_type=MESH).start()

            each_partner(send_q)

    settle(qb.at[1:nc + 1], q_r)

    @pl.when(z < nz - 1)
    def _():
        pltpu.make_async_remote_copy(
            src_ref=qb.at[nc], dst_ref=qb.at[0], send_sem=h_s.at[2], recv_sem=h_r.at[2],
            device_id=(z + 1, c), device_id_type=MESH).start()

    for s in range(nz):
        settle(xr.at[nz - 1 - s], x_r.at[s])
    lane = lax.broadcasted_iota(jnp.int32, (1, 2 * LANES), 1)
    for m in range(nz // 2):
        lags = 2 * m + 2
        even = xr[nz - 1 - 2 * m:nz - 1 - 2 * m + lags].reshape(lags * block, LANES)
        odd = xr[nz - 2 - 2 * m:nz - 2 - 2 * m + lags].reshape(lags * block, LANES)
        both = jnp.concatenate([even, odd], axis=1)
        total = None
        for g in range(groups):
            keep = ((lane // GSIZE) % groups == g).astype(F32).astype(BF16)
            term = jnp.dot(toep[g, :, 0:lags * block], both * keep, preferred_element_type=F32)
            total = term if total is None else total + term
        for i, values in enumerate((total[:, :LANES], total[:, LANES:])):
            ys[2 * m + i] = values.astype(BF16)
            p = 2 * m + i

            @pl.when(z != p)
            def _():
                pltpu.make_async_remote_copy(
                    src_ref=ys.at[p], dst_ref=yr.at[z], send_sem=y_s, recv_sem=y_r.at[z],
                    device_id=(p, c), device_id_type=MESH).start()

            @pl.when(z == p)
            def _():
                pltpu.make_async_copy(ys.at[p], yr.at[p], y_r.at[p]).start()

    @pl.when(z > 0)
    def _():
        settle(qb.at[0], h_r.at[2])

    def query_chunk(j, carry):
        s0 = j * chunk
        for h in range(halves):
            for n in range(seqs):
                ext = qb[pl.ds(s0, chunk + 1), n, :, h * LANES:(h + 1) * LANES].astype(F32)
                value = feature(ext.reshape((chunk + 1) * rows, LANES), 0, h)
                qf[pl.ds(s0, chunk), n, :, h * LANES:(h + 1) * LANES] = value.astype(BF16).reshape(
                    chunk, rows, LANES)
        return carry

    lax.fori_loop(0, chunks, query_chunk, 0)

    for h in range(halves):
        for k in range(per_half):
            settle(yr.at[halves * k + h], y_r.at[halves * k + h])

        def gate_chunk(j, carry, h=h):
            s0 = j * chunk
            t0 = pl.multiple_of(j * span, span)
            tiles = [yr[halves * k + h, pl.ds(t0, span), :].astype(F32) for k in range(per_half)]
            for n in range(seqs):
                filtered = jnp.concatenate([t[:, n * part:(n + 1) * part] for t in tiles], axis=1)
                query = qf[pl.ds(s0, chunk), n, :, h * LANES:(h + 1) * LANES].astype(F32)
                gated = query * filtered.reshape(chunk, rows, LANES)
                gs[h, pl.ds(s0, chunk), n] = gated.astype(BF16)
            return carry

        lax.fori_loop(0, chunks, gate_chunk, 0)

        def send_out(p, h=h):
            pltpu.make_async_remote_copy(
                src_ref=gs.at[h, p], dst_ref=out.at[:, :, half_cols(c, h)], send_sem=o_s, recv_sem=o_r,
                device_id=(z, p), device_id_type=MESH).start()

        each_partner(send_out)
        pltpu.make_async_copy(gs.at[h, c], out.at[:, :, half_cols(c, h)], o_r).start()

    settle(kv.at[:, 1:nc], kv_s)
    settle(qb.at[1:nc], q_s)
    settle(xs.at[1:nz], x_s)
    settle(ys.at[1:nz], y_s)

    @pl.when(z < nz - 1)
    def _():
        for h in range(halves):
            settle(kv.at[h, nc], h_s.at[h])
        settle(qb.at[nc], h_s.at[2])

    settle(gs.at[:, 1:nc], o_s)
    settle(out, o_r)


def solution(mesh):
    nz, nc = mesh.shape["seq"], mesh.shape["ch"]

    def shards(proj, short_w, long_filter):
        seqs, rows, _, width = proj.shape
        chans = width // nc
        block = rows * nc
        halves = chans // LANES
        groups, length = long_filter.shape
        own = chans // nz // GSIZE
        by_component = jnp.transpose(proj, (0, 2, 1, 3))
        dma = pltpu.SemaphoreType.DMA
        return pl.pallas_call(
            lambda *refs: kernel(nz, nc, *refs),
            out_shape=jax.ShapeDtypeStruct((seqs, rows, width), BF16),
            in_specs=[
                pl.BlockSpec(memory_space=pl.ANY),
                pl.BlockSpec(memory_space=pltpu.VMEM),
                pl.BlockSpec(memory_space=pltpu.VMEM),
            ],
            out_specs=pl.BlockSpec(memory_space=pl.ANY),
            scratch_shapes=[
                pltpu.VMEM((halves, nc + 1, seqs, 2, rows, LANES), BF16),
                pltpu.VMEM((nc + 1, seqs, rows, chans), BF16),
                pltpu.VMEM((nc, seqs, rows, chans), BF16),
                pltpu.VMEM((nz, block, LANES), BF16),
                pltpu.VMEM((nz + 1, block, LANES), BF16),
                pltpu.VMEM((nz, block, LANES), BF16),
                pltpu.VMEM((nz, block, LANES), BF16),
                pltpu.VMEM((halves, nc, seqs, rows, LANES), BF16),
                pltpu.VMEM((own, block, length), BF16),
                pltpu.VMEM((groups, length + LANES), F32),
                dma, dma((halves, nc)), dma, dma, dma((3,)), dma((3,)),
                dma, dma((nz,)), dma, dma((nz,)), dma, dma,
            ],
            compiler_params=pltpu.CompilerParams(collective_id=0, has_side_effects=True),
            name="hyena",
        )(by_component, short_w, long_filter)

    in_specs = (P(None, ("seq", "ch"), None, None), P(None, None, "ch"), P("ch", None))
    out_specs = P(None, ("seq", "ch"), None)
    return jax.shard_map(shards, mesh=mesh, in_specs=in_specs, out_specs=out_specs, check_vma=False)
```

time: 71.9 us -> 60.7 us (0.84)
  the two profiles are of different devices: /device:TPU:1 before, /device:TPU:65 now
where the time goes in v1:
time: 60.7 us; the launch traced here: 60.5 us
  Pallas kernels  58.6 us (97%)
  local copies, waits for them, and re-layouts  1.87 us (3%)
    pallas_call x1, Pallas kernels, shards(): pl.pallas_call(lambda *refs: kernel(nz, nc, *refs), out_shape=jax.ShapeDt...  58.6 us
    unnamed x1, local copies, waits for them, and re-layouts  1.87 us

profile of v1, /device:TPU:65, one launch (start us, length us, event | category | flops | bytes accessed | tf_op | source)
XLA Modules:
  0.0 60.5 jit_solution(5237658922995497171)
XLA Ops:
  0.0 58.6 %hyena.1 = bf16[4,8,8192]{2,1,0:T(8,128)(2,1)} custom-call(bf16[4,3,8,8192]{3,2,1,0:T(8,128)(2,1)} %bitcast.1, f32[3,3,256]{2,1,0:T(4,128)} %refs_1_.1, bf16[16,2048]{1,0:T(8,128)(2,1)} %refs_2_.1), custom_call_target="tpu_custom_call" | custom-call | tf_op jit(solution)/shard_map/hyena/pallas_call | solution.py:286
  58.6 1.9 %copy.5 = bf16[4,8,8192]{2,1,0:T(8,128)(2,1)} copy(bf16[4,8,8192]{2,1,0:T(8,128)(2,1)} %hyena.1) | data formatting | bytes 1048576

commit v2 on v1

v2 whole, which is shorter than its diff:
```python
import jax
import jax.numpy as jnp
from jax import lax
from jax.experimental import pallas as pl
from jax.experimental.pallas import tpu as pltpu
from jax.sharding import PartitionSpec as P

MESH = pl.DeviceIdType.MESH
GSIZE = 16
LANES = 128
F32 = jnp.float32
BF16 = jnp.bfloat16


def kernel(nz, nc, proj_in, w_in, lf_in, out, proj, w_ref, lf_ref, kv, qb, qf, xs, xr, xu, wl, ys, yr, gs, toep, rev,
           in_r, kv_s, kv_r, q_s, q_r, h_s, h_r, x_s, x_r, y_s, y_r, o_s, o_r):
    z = lax.axis_index("seq")
    c = lax.axis_index("ch")
    seqs, _, rows, _ = proj.shape
    halves, pairs, chans = kv.shape[0], kv.shape[1], qb.shape[-1]
    duo = seqs // pairs
    block = rows * nc
    part = chans // nz
    per_half = LANES // part
    taps = w_ref.shape[0]
    chunk = 8
    chunks = nc // chunk
    span = chunk * rows
    folds = block // LANES
    fold_slots = nc // folds
    strips = fold_slots // chunk
    own_half = lax.rem(z, halves)
    side = 4
    around = (2, 1, 3, 0)
    line = (4, 3, 5, 2, 6, 1, 7)

    def cols(p):
        return pl.ds(pl.multiple_of(p * chans, chans), chans)

    def half_cols(p, h):
        return pl.ds(pl.multiple_of(p * chans + h * LANES, LANES), LANES)

    def settle(ref, sem):
        pltpu.make_async_copy(ref, ref, sem).wait()

    across = [lax.rem(c // 8 + d, side) * 8 for d in range(side)]
    along = [lax.rem(c // 2 + d, side) * 2 for d in range(side)]
    core = [lax.rem(c + d, 2) for d in range(2)]

    def each_partner(body):
        for dx in around:
            for dy in around:
                for dc in (1, 0):
                    if (dx, dy, dc) != (0, 0, 0):
                        body(across[dx] + along[dy] + core[dc])

    barrier = pltpu.get_barrier_semaphore()

    def greet(p):
        pl.semaphore_signal(barrier, inc=1, device_id=(z, p), device_id_type=MESH)

    for n in range(seqs):
        pltpu.make_async_copy(proj_in.at[n], proj.at[n], in_r.at[0]).start()
    pltpu.make_async_copy(lf_in, lf_ref, in_r.at[1]).start()
    pltpu.make_async_copy(w_in, w_ref, in_r.at[2]).start()
    each_partner(greet)
    for d in line:
        pl.semaphore_signal(barrier, inc=1, device_id=(lax.rem(z + d, nz), c), device_id_type=MESH)
    settle(proj, in_r.at[0])
    last = c // (nc - 1)
    for h in range(halves):
        for a in range(pairs):
            pltpu.make_async_copy(
                proj.at[a * duo:(a + 1) * duo, 1:3, :, half_cols(c, h)], kv.at[h, a, c + 1],
                kv_r.at[h, a]).start()
    pltpu.make_async_copy(proj.at[:, 0, :, cols(c)], qb.at[c + 1], q_r.at[last]).start()
    pl.semaphore_wait(barrier, nc - 1 + nz - 1)

    for h in range(halves):
        for a in range(pairs):
            def send_kv(p, h=h, a=a):
                pltpu.make_async_remote_copy(
                    src_ref=proj.at[a * duo:(a + 1) * duo, 1:3, :, half_cols(p, h)],
                    dst_ref=kv.at[h, a, c + 1], send_sem=kv_s, recv_sem=kv_r.at[h, a],
                    device_id=(z, p), device_id_type=MESH).start()

            each_partner(send_kv)

    settle(lf_ref, in_r.at[1])
    settle(w_ref, in_r.at[2])

    length = lf_ref.shape[1]
    pieces = length // LANES
    flip = (lax.broadcasted_iota(jnp.int32, (LANES, LANES), 0)
            + lax.broadcasted_iota(jnp.int32, (LANES, LANES), 1)) == LANES - 1
    flip = flip.astype(F32).astype(BF16)
    rev[:, 0:LANES] = jnp.zeros((lf_ref.shape[0], LANES), F32)
    for m in range(pieces):
        rev[:, (m + 1) * LANES:(m + 2) * LANES] = jnp.dot(
            lf_ref[:, m * LANES:(m + 1) * LANES], flip, preferred_element_type=F32)
    groups = part // GSIZE
    own_row = (own_half * LANES + (z // halves) * part) // GSIZE
    for g in range(groups):
        for m in range(pieces):
            pair = rev[pl.ds(own_row + g, 1), m * LANES:(m + 2) * LANES]
            pair = jnp.broadcast_to(pair, (LANES, 2 * LANES))
            tile = pltpu.roll(pair, 1, 1, stride=1, stride_axis=0)[:, :LANES]
            tile = tile.astype(BF16)
            for th in range(2):
                for sh in range(2):
                    twice = m - th + sh
                    if twice % 2 == 0 and 0 <= twice // 2 < nz:
                        base = (twice // 2) * block + sh * LANES
                        toep[g, th * LANES:(th + 1) * LANES, base:base + LANES] = tile
        toep[g, 0:LANES, LANES:2 * LANES] = jnp.zeros((LANES, LANES), BF16)

    for k in range(taps):
        for i in range(2):
            mine = jnp.where(own_half == 0, w_ref[k, i + 1:i + 2, :LANES], w_ref[k, i + 1:i + 2, LANES:])
            mine = pltpu.roll(jnp.broadcast_to(mine, (rows, LANES)), LANES - (z // halves) * part, 1)
            wl[k, i] = jnp.concatenate([mine[:, :part]] * seqs, axis=1)

    xu[nz] = jnp.zeros(xu.shape[1:], BF16)
    row = lax.broadcasted_iota(jnp.int32, (rows, LANES), 0)
    for h in range(halves):
        for a in range(pairs):
            kv[h, a, 0] = jnp.zeros(kv.shape[3:], BF16)

    @pl.when(z == 0)
    def _():
        qb[0] = jnp.zeros(qb.shape[1:], BF16)

    def feature(ext, i, h):
        total = None
        for k in range(taps):
            term = w_ref[k, i:i + 1, h * LANES:(h + 1) * LANES] * ext[rows - k:rows - k + span]
            total = term if total is None else total + term
        return total

    def send_q(p):
        pltpu.make_async_remote_copy(
            src_ref=proj.at[:, 0, :, cols(p)], dst_ref=qb.at[c + 1], send_sem=q_s,
            recv_sem=q_r.at[last], device_id=(z, p), device_id_type=MESH).start()

    for h in range(halves):
        for a in range(pairs):
            settle(kv.at[h, a, 1:nc + 1], kv_r.at[h, a])

            def product_strip(k, carry, h=h, a=a):
                j = strips - 1 - k

                prods = []
                for f in range(folds):
                    for n in range(duo):
                        feats = []
                        for i in range(2):
                            ext = kv[h, a, pl.ds(f * fold_slots + j * chunk, chunk + 1), n, i].astype(F32)
                            feats.append(feature(ext.reshape((chunk + 1) * rows, LANES), i + 1, h))
                        prods.append(feats[0] * feats[1])
                t0 = pl.multiple_of(j * span, span)
                for k in range(per_half):
                    tile = jnp.concatenate([p[:, k * part:(k + 1) * part] for p in prods], axis=1)
                    xs[halves * k + h, a, pl.ds(t0, span), :] = tile.astype(BF16)
                return carry

            lax.fori_loop(0, strips, product_strip, 0)

            rims = []
            for n in range(duo):
                rim = pltpu.roll(kv[h, a, 1, n, 1].astype(F32), 6, 0)
                rim = jnp.where(row < 6, pltpu.roll(kv[h, a, 1, n, 0].astype(F32), 4, 0), rim)
                rim = jnp.where(row < 4, pltpu.roll(kv[h, a, nc, n, 1].astype(F32), 4, 0), rim)
                rims.append(jnp.where(row < 2, pltpu.roll(kv[h, a, nc, n, 0].astype(F32), 2, 0), rim))
            for k in range(per_half):
                tile = jnp.concatenate([r[:, k * part:(k + 1) * part] for r in rims * folds], axis=1)
                xs[halves * k + h, a, LANES:LANES + rows, :] = tile.astype(BF16)

            for d in (2, 1, 3, 0):
                p = halves * lax.rem(z // halves + d, per_half) + h

                def send_x(p=p, a=a):
                    pltpu.make_async_remote_copy(
                        src_ref=xs.at[p, a], dst_ref=xr.at[z, a], send_sem=x_s, recv_sem=x_r.at[z, a],
                        device_id=(p, c), device_id_type=MESH).start()

                if d > 0:
                    send_x()
                else:
                    pl.when(own_half != h)(send_x)

            if (h, a) == (halves - 1, 0):
                each_partner(send_q)

            @pl.when(own_half == h)
            def _():
                pltpu.make_async_copy(xs.at[z, a], xr.at[z, a], x_r.at[z, a]).start()

    def pass_query_rim():
        settle(qb.at[nc], q_r.at[1])

        @pl.when(z < nz - 1)
        def _():
            pltpu.make_async_remote_copy(
                src_ref=qb.at[nc], dst_ref=qb.at[0], send_sem=h_s, recv_sem=h_r,
                device_id=(z + 1, c), device_id_type=MESH).start()

    pl.when(own_half != 0)(pass_query_rim)

    before = None
    for s in range(nz):
        tiles, rims = [], []
        for a in range(pairs):
            settle(xr.at[s, a], x_r.at[s, a])
            tiles.append(xr[s, a, :LANES, :])
            rims.append(xr[s, a, LANES:LANES + rows, :].astype(F32)[:, :LANES // pairs])
        for f in range(folds):
            at = f * LANES // folds
            xu[nz - 1 - s, f * LANES:(f + 1) * LANES, :] = jnp.concatenate(
                [t[:, at:at + LANES // folds] for t in tiles], axis=1)
        rim = jnp.concatenate(rims, axis=1)
        if s > 0:
            firsts, seconds = [], []
            for i in range(2):
                t0, t1 = rim[4 + 2 * i:5 + 2 * i], rim[5 + 2 * i:6 + 2 * i]
                b2, b1 = before[2 * i:2 * i + 1], before[2 * i + 1:2 * i + 2]
                w0, w1, w2 = wl[0, i, 0:1], wl[1, i, 0:1], wl[2, i, 0:1]
                firsts.append(w0 * t0 + w1 * b1 + w2 * b2)
                seconds.append(w0 * t1 + w1 * t0 + w2 * b1)
            head = xu[nz - 1 - s, 0:2 * rows, :].astype(F32)
            at = lax.broadcasted_iota(jnp.int32, head.shape, 0)
            head = jnp.where(at == 0, firsts[0] * firsts[1], head)
            head = jnp.where(at == 1, seconds[0] * seconds[1], head)
            xu[nz - 1 - s, 0:2 * rows, :] = head.astype(BF16)
        before = rim

    lane = lax.broadcasted_iota(jnp.int32, (1, 2 * LANES), 1)
    for m in range(nz // 2):
        lags = 2 * m + 2
        even = xu[nz - 1 - 2 * m:nz - 1 - 2 * m + lags].reshape(lags * block, LANES)
        odd = xu[nz - 2 - 2 * m:nz - 2 - 2 * m + lags].reshape(lags * block, LANES)
        both = jnp.concatenate([even, odd], axis=1)
        total = None
        for g in range(groups):
            keep = ((lane // GSIZE) % groups == g).astype(F32).astype(BF16)
            term = jnp.dot(toep[g, :, 0:lags * block], both * keep, preferred_element_type=F32)
            total = term if total is None else total + term
        ys[2 * m] = total[:, :LANES].astype(BF16)
        ys[2 * m + 1] = total[:, LANES:].astype(BF16)

    for d in line:
        p = lax.rem(z + d, nz)
        pltpu.make_async_remote_copy(
            src_ref=ys.at[p], dst_ref=yr.at[z], send_sem=y_s, recv_sem=y_r.at[z],
            device_id=(p, c), device_id_type=MESH).start()
    pltpu.make_async_copy(ys.at[z], yr.at[z], y_r.at[z]).start()

    pl.when(own_half == 0)(pass_query_rim)
    settle(qb.at[1:nc], q_r.at[0])

    @pl.when(z > 0)
    def _():
        settle(qb.at[0], h_r)

    def query_chunk(j, carry):
        s0 = j * chunk
        for h in range(halves):
            for n in range(seqs):
                ext = qb[pl.ds(s0, chunk + 1), n, :, h * LANES:(h + 1) * LANES].astype(F32)
                value = feature(ext.reshape((chunk + 1) * rows, LANES), 0, h)
                qf[pl.ds(s0, chunk), n, :, h * LANES:(h + 1) * LANES] = value.astype(BF16).reshape(
                    chunk, rows, LANES)
        return carry

    lax.fori_loop(0, chunks, query_chunk, 0)

    for h in range(halves):
        for k in range(per_half):
            settle(yr.at[halves * k + h], y_r.at[halves * k + h])

        def gate_chunk(j, carry, h=h):
            s0 = j * chunk
            t0 = pl.multiple_of(j * span, span)
            tiles = [yr[halves * k + h, pl.ds(t0, span), :].astype(F32) for k in range(per_half)]
            for n in range(seqs):
                filtered = jnp.concatenate([t[:, n * part:(n + 1) * part] for t in tiles], axis=1)
                query = qf[pl.ds(s0, chunk), n, :, h * LANES:(h + 1) * LANES].astype(F32)
                gated = query * filtered.reshape(chunk, rows, LANES)
                gs[h, pl.ds(s0, chunk), n] = gated.astype(BF16)
            return carry

        lax.fori_loop(0, chunks, gate_chunk, 0)

        def send_out(p, h=h):
            pltpu.make_async_remote_copy(
                src_ref=gs.at[h, p], dst_ref=out.at[:, :, half_cols(c, h)], send_sem=o_s, recv_sem=o_r,
                device_id=(z, p), device_id_type=MESH).start()

        each_partner(send_out)
        pltpu.make_async_copy(gs.at[h, c], out.at[:, :, half_cols(c, h)], o_r).start()

    settle(kv.at[:, :, 1:nc], kv_s)
    settle(qb.at[1:nc], q_s)
    settle(xs.at[1:nz], x_s)
    settle(ys.at[1:nz], y_s)

    @pl.when(z < nz - 1)
    def _():
        settle(qb.at[nc], h_s)

    settle(gs.at[:, 1:nc], o_s)
    settle(out, o_r)


def solution(mesh):
    nz, nc = mesh.shape["seq"], mesh.shape["ch"]

    def shards(proj, short_w, long_filter):
        seqs, rows, _, width = proj.shape
        chans = width // nc
        block = rows * nc
        halves = chans // LANES
        part = chans // nz
        pairs = seqs * part // LANES * (block // LANES)
        groups, length = long_filter.shape
        own = part // GSIZE
        by_component = jnp.transpose(proj, (0, 2, 1, 3))
        dma = pltpu.SemaphoreType.DMA
        sources = pltpu.VMEM((nz, pairs, LANES + rows, LANES), BF16)
        results = pltpu.VMEM((nz, block, LANES), BF16)
        duo = seqs // pairs
        return pl.pallas_call(
            lambda *refs: kernel(nz, nc, *refs),
            out_shape=jax.ShapeDtypeStruct((seqs, rows, width), BF16),
            in_specs=[pl.BlockSpec(memory_space=pl.ANY)] * 3,
            out_specs=pl.BlockSpec(memory_space=pl.ANY),
            scratch_shapes=[
                pltpu.VMEM((seqs, 3, rows, width), BF16),
                pltpu.VMEM(short_w.shape, F32),
                pltpu.VMEM(long_filter.shape, BF16),
                pltpu.VMEM((halves, pairs, nc + 1, duo, 2, rows, LANES), BF16),
                pltpu.VMEM((nc + 1, seqs, rows, chans), BF16),
                pltpu.VMEM((nc, seqs, rows, chans), BF16),
                sources, sources,
                pltpu.VMEM((nz + 1, block, LANES), BF16),
                pltpu.VMEM((short_w.shape[0], 2, rows, LANES), F32),
                results, results,
                pltpu.VMEM((halves, nc, seqs, rows, LANES), BF16),
                pltpu.VMEM((own, block, length), BF16),
                pltpu.VMEM((groups, length + LANES), F32),
                dma((3,)), dma, dma((halves, pairs)), dma, dma((2,)), dma, dma,
                dma, dma((nz, pairs)), dma, dma((nz,)), dma, dma,
            ],
            compiler_params=pltpu.CompilerParams(collective_id=0, has_side_effects=True),
            name="hyena",
        )(by_component, short_w, long_filter)

    in_specs = (P(None, ("seq", "ch"), None, None), P(None, None, "ch"), P("ch", None))
    out_specs = P(None, ("seq", "ch"), None)
    return jax.shard_map(shards, mesh=mesh, in_specs=in_specs, out_specs=out_specs, check_vma=False)
```

time: 60.7 us -> 54.5 us (0.90)
  the two profiles are of different devices: /device:TPU:65 before, /device:TPU:1 now
where the time goes in v2:
time: 54.5 us; the launch traced here: 54.4 us
  Pallas kernels  52.5 us (96%)
  local copies, waits for them, and re-layouts  1.87 us (3%)
    pallas_call x1, Pallas kernels, shards(): pl.pallas_call(lambda *refs: kernel(nz, nc, *refs), out_shape=jax.ShapeDt...  52.5 us
    unnamed x1, local copies, waits for them, and re-layouts  1.87 us

profile of v2, /device:TPU:1, one launch (start us, length us, event | category | flops | bytes accessed | tf_op | source)
XLA Modules:
  0.0 54.4 jit_solution(5626924813674771798)
XLA Ops:
  0.0 52.5 %hyena.1 = bf16[4,8,8192]{2,1,0:T(8,128)(2,1)} custom-call(bf16[4,3,8,8192]{3,2,1,0:T(8,128)(2,1)} %bitcast.1, f32[3,3,256]{2,1,0:T(4,128)} %refs_1_.1, bf16[16,2048]{1,0:T(8,128)(2,1)} %refs_2_.1), custom_call_target="tpu_custom_call" | custom-call | tf_op jit(solution)/shard_map/hyena/pallas_call | solution.py:331
  52.5 1.9 %copy.5 = bf16[4,8,8192]{2,1,0:T(8,128)(2,1)} copy(bf16[4,8,8192]{2,1,0:T(8,128)(2,1)} %hyena.1) | data formatting | bytes 1048576

commit v3 on v2

--- a/solution.py
+++ b/solution.py
@@ -12,7 +12,7 @@
 BF16 = jnp.bfloat16
 
 
-def kernel(nz, nc, proj_in, w_in, lf_in, out, proj, w_ref, lf_ref, kv, qb, qf, xs, xr, xu, wl, ys, yr, gs, toep, rev,
+def kernel(nz, nc, proj_in, w_in, lf_in, out, proj, w_ref, lf_ref, kv, qb, qf, xs, xr, xu, edge, wl, ys, yr, gs, toep, rev,
            in_r, kv_s, kv_r, q_s, q_r, h_s, h_r, x_s, x_r, y_s, y_r, o_s, o_r):
     z = lax.axis_index("seq")
     c = lax.axis_index("ch")
@@ -29,7 +29,8 @@
     folds = block // LANES
     fold_slots = nc // folds
     strips = fold_slots // chunk
-    own_half = lax.rem(z, halves)
+    own_half = lax.rem(z + c, halves)
+    parity = [lax.rem(h + c, halves) for h in range(halves)]
     side = 4
     around = (2, 1, 3, 0)
     line = (4, 3, 5, 2, 6, 1, 7)
@@ -160,7 +161,7 @@
                 t0 = pl.multiple_of(j * span, span)
                 for k in range(per_half):
                     tile = jnp.concatenate([p[:, k * part:(k + 1) * part] for p in prods], axis=1)
-                    xs[halves * k + h, a, pl.ds(t0, span), :] = tile.astype(BF16)
+                    xs[halves * k + parity[h], a, pl.ds(t0, span), :] = tile.astype(BF16)
                 return carry
 
             lax.fori_loop(0, strips, product_strip, 0)
@@ -173,10 +174,10 @@
                 rims.append(jnp.where(row < 2, pltpu.roll(kv[h, a, nc, n, 0].astype(F32), 2, 0), rim))
             for k in range(per_half):
                 tile = jnp.concatenate([r[:, k * part:(k + 1) * part] for r in rims * folds], axis=1)
-                xs[halves * k + h, a, LANES:LANES + rows, :] = tile.astype(BF16)
+                xs[halves * k + parity[h], a, LANES:LANES + rows, :] = tile.astype(BF16)
 
             for d in (2, 1, 3, 0):
-                p = halves * lax.rem(z // halves + d, per_half) + h
+                p = halves * lax.rem(z // halves + d, per_half) + parity[h]
 
                 def send_x(p=p, a=a):
                     pltpu.make_async_remote_copy(
@@ -195,43 +196,34 @@
             def _():
                 pltpu.make_async_copy(xs.at[z, a], xr.at[z, a], x_r.at[z, a]).start()
 
-    def pass_query_rim():
-        settle(qb.at[nc], q_r.at[1])
-
-        @pl.when(z < nz - 1)
-        def _():
-            pltpu.make_async_remote_copy(
-                src_ref=qb.at[nc], dst_ref=qb.at[0], send_sem=h_s, recv_sem=h_r,
-                device_id=(z + 1, c), device_id_type=MESH).start()
-
-    pl.when(own_half != 0)(pass_query_rim)
-
-    before = None
     for s in range(nz):
-        tiles, rims = [], []
         for a in range(pairs):
             settle(xr.at[s, a], x_r.at[s, a])
-            tiles.append(xr[s, a, :LANES, :])
-            rims.append(xr[s, a, LANES:LANES + rows, :].astype(F32)[:, :LANES // pairs])
+    for s in range(nz):
+        tiles = [xr[s, a, :LANES, :] for a in range(pairs)]
+        rims = [xr[s, a, LANES:LANES + rows, :].astype(F32)[:, :LANES // pairs] for a in range(pairs)]
         for f in range(folds):
             at = f * LANES // folds
             xu[nz - 1 - s, f * LANES:(f + 1) * LANES, :] = jnp.concatenate(
                 [t[:, at:at + LANES // folds] for t in tiles], axis=1)
-        rim = jnp.concatenate(rims, axis=1)
-        if s > 0:
-            firsts, seconds = [], []
-            for i in range(2):
-                t0, t1 = rim[4 + 2 * i:5 + 2 * i], rim[5 + 2 * i:6 + 2 * i]
-                b2, b1 = before[2 * i:2 * i + 1], before[2 * i + 1:2 * i + 2]
-                w0, w1, w2 = wl[0, i, 0:1], wl[1, i, 0:1], wl[2, i, 0:1]
-                firsts.append(w0 * t0 + w1 * b1 + w2 * b2)
-                seconds.append(w0 * t1 + w1 * t0 + w2 * b1)
-            head = xu[nz - 1 - s, 0:2 * rows, :].astype(F32)
-            at = lax.broadcasted_iota(jnp.int32, head.shape, 0)
-            head = jnp.where(at == 0, firsts[0] * firsts[1], head)
-            head = jnp.where(at == 1, seconds[0] * seconds[1], head)
-            xu[nz - 1 - s, 0:2 * rows, :] = head.astype(BF16)
-        before = rim
+        edge[s] = jnp.concatenate(rims, axis=1)
+
+    firsts, seconds = [], []
+    for i in range(2):
+        b2, b1 = edge[:, 2 * i, :], edge[:, 2 * i + 1, :]
+        t0, t1 = edge[:, 4 + 2 * i, :], edge[:, 5 + 2 * i, :]
+        block_row = lax.broadcasted_iota(jnp.int32, b2.shape, 0)
+        b2 = jnp.where(block_row == 0, 0.0, pltpu.roll(b2, 1, 0))
+        b1 = jnp.where(block_row == 0, 0.0, pltpu.roll(b1, 1, 0))
+        w0, w1, w2 = wl[0, i], wl[1, i], wl[2, i]
+        firsts.append(w0 * t0 + w1 * b1 + w2 * b2)
+        seconds.append(w0 * t1 + w1 * t0 + w2 * b1)
+    first, second = firsts[0] * firsts[1], seconds[0] * seconds[1]
+    for s in range(1, nz):
+        head = xu[nz - 1 - s, 0:2 * rows, :].astype(F32)
+        at = lax.broadcasted_iota(jnp.int32, head.shape, 0)
+        head = jnp.where(at == 0, first[s:s + 1], jnp.where(at == 1, second[s:s + 1], head))
+        xu[nz - 1 - s, 0:2 * rows, :] = head.astype(BF16)
 
     lane = lax.broadcasted_iota(jnp.int32, (1, 2 * LANES), 1)
     for m in range(nz // 2):
@@ -246,15 +238,24 @@
             total = term if total is None else total + term
         ys[2 * m] = total[:, :LANES].astype(BF16)
         ys[2 * m + 1] = total[:, LANES:].astype(BF16)
-
-    for d in line:
-        p = lax.rem(z + d, nz)
-        pltpu.make_async_remote_copy(
-            src_ref=ys.at[p], dst_ref=yr.at[z], send_sem=y_s, recv_sem=y_r.at[z],
-            device_id=(p, c), device_id_type=MESH).start()
+        if m == 1:
+            settle(qb.at[nc], q_r.at[1])
+
+            @pl.when(z < nz - 1)
+            def _():
+                pltpu.make_async_remote_copy(
+                    src_ref=qb.at[nc], dst_ref=qb.at[0], send_sem=h_s, recv_sem=h_r,
+                    device_id=(z + 1, c), device_id_type=MESH).start()
+
+        if m % 2 == 1:
+            for p in range(2 * m - 2, 2 * m + 2):
+                @pl.when(z != p)
+                def _(p=p):
+                    pltpu.make_async_remote_copy(
+                        src_ref=ys.at[p], dst_ref=yr.at[z], send_sem=y_s, recv_sem=y_r.at[z],
+                        device_id=(p, c), device_id_type=MESH).start()
     pltpu.make_async_copy(ys.at[z], yr.at[z], y_r.at[z]).start()
 
-    pl.when(own_half == 0)(pass_query_rim)
     settle(qb.at[1:nc], q_r.at[0])
 
     @pl.when(z > 0)
@@ -275,12 +276,12 @@
 
     for h in range(halves):
         for k in range(per_half):
-            settle(yr.at[halves * k + h], y_r.at[halves * k + h])
+            settle(yr.at[halves * k + parity[h]], y_r.at[halves * k + parity[h]])
 
         def gate_chunk(j, carry, h=h):
             s0 = j * chunk
             t0 = pl.multiple_of(j * span, span)
-            tiles = [yr[halves * k + h, pl.ds(t0, span), :].astype(F32) for k in range(per_half)]
+            tiles = [yr[halves * k + parity[h], pl.ds(t0, span), :].astype(F32) for k in range(per_half)]
             for n in range(seqs):
                 filtered = jnp.concatenate([t[:, n * part:(n + 1) * part] for t in tiles], axis=1)
                 query = qf[pl.ds(s0, chunk), n, :, h * LANES:(h + 1) * LANES].astype(F32)
@@ -330,8 +331,8 @@
         duo = seqs // pairs
         return pl.pallas_call(
             lambda *refs: kernel(nz, nc, *refs),
-            out_shape=jax.ShapeDtypeStruct((seqs, rows, width), BF16),
-            in_specs=[pl.BlockSpec(memory_space=pl.ANY)] * 3,
+            out_shape=pltpu.VMEM((seqs, rows, width), BF16),
+            in_specs=[pl.BlockSpec(memory_space=pltpu.HBM)] * 3,
             out_specs=pl.BlockSpec(memory_space=pl.ANY),
             scratch_shapes=[
                 pltpu.VMEM((seqs, 3, rows, width), BF16),
@@ -342,6 +343,7 @@
                 pltpu.VMEM((nc, seqs, rows, chans), BF16),
                 sources, sources,
                 pltpu.VMEM((nz + 1, block, LANES), BF16),
+                pltpu.VMEM((nz, rows, LANES), F32),
                 pltpu.VMEM((short_w.shape[0], 2, rows, LANES), F32),
                 results, results,
                 pltpu.VMEM((halves, nc, seqs, rows, LANES), BF16),

time: 54.5 us -> 51 us (0.936)
  the two profiles are of different devices: /device:TPU:1 before, /device:TPU:66 now
where the time goes in v3:
time: 51 us; the launch traced here: 50.9 us
  Pallas kernels  50.1 us (98%)
  local copies, waits for them, and re-layouts  0.8 us (2%)
    pallas_call x1, Pallas kernels, shards(): pl.pallas_call(lambda *refs: kernel(nz, nc, *refs), out_shape=pltpu.VMEM(...  50.1 us

profile of v3, /device:TPU:66, one launch (start us, length us, event | category | flops | bytes accessed | tf_op | source)
XLA Modules:
  0.0 50.9 jit_solution(16370563395551809861)
XLA Ops:
  0.0 50.1 %hyena.1 = bf16[4,8,8192]{2,1,0:T(8,128)(2,1)S(1)} custom-call(bf16[4,3,8,8192]{3,2,1,0:T(8,128)(2,1)} %bitcast.1, f32[3,3,256]{2,1,0:T(4,128)} %refs_1_.1, bf16[16,2048]{1,0:T(8,128)(2,1)} %refs_2_.1), custom_call_target="tpu_custom_call" | custom-call | tf_op jit(solution)/shard_map/hyena/pallas_call | solution.py:332
  50.1 0.8 %copy.5 = bf16[4,8,8192]{2,1,0:T(8,128)(2,1)} copy(bf16[4,8,8192]{2,1,0:T(8,128)(2,1)S(1)} %hyena.1) | data formatting | bytes 1048576

commit v4 on v3

--- a/solution.py
+++ b/solution.py
@@ -166,22 +166,26 @@
 
             lax.fori_loop(0, strips, product_strip, 0)
 
-            rims = []
-            for n in range(duo):
-                rim = pltpu.roll(kv[h, a, 1, n, 1].astype(F32), 6, 0)
-                rim = jnp.where(row < 6, pltpu.roll(kv[h, a, 1, n, 0].astype(F32), 4, 0), rim)
-                rim = jnp.where(row < 4, pltpu.roll(kv[h, a, nc, n, 1].astype(F32), 4, 0), rim)
-                rims.append(jnp.where(row < 2, pltpu.roll(kv[h, a, nc, n, 0].astype(F32), 2, 0), rim))
-            for k in range(per_half):
-                tile = jnp.concatenate([r[:, k * part:(k + 1) * part] for r in rims * folds], axis=1)
-                xs[halves * k + parity[h], a, LANES:LANES + rows, :] = tile.astype(BF16)
+            tall = LANES
+            if a == pairs - 1:
+                tall = LANES + rows
+                rims = []
+                for n in range(seqs):
+                    head, tail = kv.at[h, n // duo, 1, n % duo], kv.at[h, n // duo, nc, n % duo]
+                    rim = pltpu.roll(head[1].astype(F32), 6, 0)
+                    rim = jnp.where(row < 6, pltpu.roll(head[0].astype(F32), 4, 0), rim)
+                    rim = jnp.where(row < 4, pltpu.roll(tail[1].astype(F32), 4, 0), rim)
+                    rims.append(jnp.where(row < 2, pltpu.roll(tail[0].astype(F32), 2, 0), rim))
+                for k in range(per_half):
+                    tile = jnp.concatenate([r[:, k * part:(k + 1) * part] for r in rims], axis=1)
+                    xs[halves * k + parity[h], a, LANES:LANES + rows, :] = tile.astype(BF16)
 
             for d in (2, 1, 3, 0):
                 p = halves * lax.rem(z // halves + d, per_half) + parity[h]
 
-                def send_x(p=p, a=a):
+                def send_x(p=p, a=a, tall=tall):
                     pltpu.make_async_remote_copy(
-                        src_ref=xs.at[p, a], dst_ref=xr.at[z, a], send_sem=x_s, recv_sem=x_r.at[z, a],
+                        src_ref=xs.at[p, a, 0:tall], dst_ref=xr.at[z, a, 0:tall], send_sem=x_s, recv_sem=x_r.at[z, a],
                         device_id=(p, c), device_id_type=MESH).start()
 
                 if d > 0:
@@ -194,19 +198,30 @@
 
             @pl.when(own_half == h)
             def _():
-                pltpu.make_async_copy(xs.at[z, a], xr.at[z, a], x_r.at[z, a]).start()
+                pltpu.make_async_copy(
+                    xs.at[z, a, 0:tall], xr.at[z, a, 0:tall], x_r.at[z, a]).start()
+
+    def pass_query_rim():
+        settle(qb.at[nc], q_r.at[1])
+
+        @pl.when(z < nz - 1)
+        def _():
+            pltpu.make_async_remote_copy(
+                src_ref=qb.at[nc], dst_ref=qb.at[0], send_sem=h_s, recv_sem=h_r,
+                device_id=(z + 1, c), device_id_type=MESH).start()
+
+    pl.when(own_half != 0)(pass_query_rim)
 
     for s in range(nz):
         for a in range(pairs):
-            settle(xr.at[s, a], x_r.at[s, a])
+            settle(xr.at[s, a, 0:LANES + rows * (a // (pairs - 1))], x_r.at[s, a])
     for s in range(nz):
         tiles = [xr[s, a, :LANES, :] for a in range(pairs)]
-        rims = [xr[s, a, LANES:LANES + rows, :].astype(F32)[:, :LANES // pairs] for a in range(pairs)]
         for f in range(folds):
             at = f * LANES // folds
             xu[nz - 1 - s, f * LANES:(f + 1) * LANES, :] = jnp.concatenate(
                 [t[:, at:at + LANES // folds] for t in tiles], axis=1)
-        edge[s] = jnp.concatenate(rims, axis=1)
+        edge[s] = xr[s, pairs - 1, LANES:LANES + rows, :].astype(F32)
 
     firsts, seconds = [], []
     for i in range(2):
@@ -226,6 +241,14 @@
         xu[nz - 1 - s, 0:2 * rows, :] = head.astype(BF16)
 
     lane = lax.broadcasted_iota(jnp.int32, (1, 2 * LANES), 1)
+
+    def send_y(p, e):
+        @pl.when(z != p)
+        def _():
+            pltpu.make_async_remote_copy(
+                src_ref=ys.at[p, e], dst_ref=yr.at[z, e], send_sem=y_s, recv_sem=y_r.at[z, e],
+                device_id=(p, c), device_id_type=MESH).start()
+
     for m in range(nz // 2):
         lags = 2 * m + 2
         even = xu[nz - 1 - 2 * m:nz - 1 - 2 * m + lags].reshape(lags * block, LANES)
@@ -236,25 +259,20 @@
             keep = ((lane // GSIZE) % groups == g).astype(F32).astype(BF16)
             term = jnp.dot(toep[g, :, 0:lags * block], both * keep, preferred_element_type=F32)
             total = term if total is None else total + term
-        ys[2 * m] = total[:, :LANES].astype(BF16)
-        ys[2 * m + 1] = total[:, LANES:].astype(BF16)
-        if m == 1:
-            settle(qb.at[nc], q_r.at[1])
-
-            @pl.when(z < nz - 1)
-            def _():
-                pltpu.make_async_remote_copy(
-                    src_ref=qb.at[nc], dst_ref=qb.at[0], send_sem=h_s, recv_sem=h_r,
-                    device_id=(z + 1, c), device_id_type=MESH).start()
-
+        for i in range(2):
+            result = total[:, i * LANES:(i + 1) * LANES].astype(BF16)
+            result = result.reshape(nc // 2, 2, rows, LANES)
+            for e in range(2):
+                ys[2 * m + i, e] = result[:, e]
+        if m == nz // 2 - 1:
+            pl.when(own_half == 0)(pass_query_rim)
         if m % 2 == 1:
             for p in range(2 * m - 2, 2 * m + 2):
-                @pl.when(z != p)
-                def _(p=p):
-                    pltpu.make_async_remote_copy(
-                        src_ref=ys.at[p], dst_ref=yr.at[z], send_sem=y_s, recv_sem=y_r.at[z],
-                        device_id=(p, c), device_id_type=MESH).start()
-    pltpu.make_async_copy(ys.at[z], yr.at[z], y_r.at[z]).start()
+                send_y(p, 0)
+    for p in range(nz):
+        send_y(p, 1)
+    for e in range(2):
+        pltpu.make_async_copy(ys.at[z, e], yr.at[z, e], y_r.at[z, e]).start()
 
     settle(qb.at[1:nc], q_r.at[0])
 
@@ -268,47 +286,64 @@
             for n in range(seqs):
                 ext = qb[pl.ds(s0, chunk + 1), n, :, h * LANES:(h + 1) * LANES].astype(F32)
                 value = feature(ext.reshape((chunk + 1) * rows, LANES), 0, h)
-                qf[pl.ds(s0, chunk), n, :, h * LANES:(h + 1) * LANES] = value.astype(BF16).reshape(
-                    chunk, rows, LANES)
+                value = value.astype(BF16).reshape(chunk // 2, 2, rows, LANES)
+                for e in range(2):
+                    qf[e, pl.ds(j * (chunk // 2), chunk // 2), n, :, h * LANES:(h + 1) * LANES] = value[:, e]
         return carry
 
     lax.fori_loop(0, chunks, query_chunk, 0)
 
     for h in range(halves):
-        for k in range(per_half):
-            settle(yr.at[halves * k + parity[h]], y_r.at[halves * k + parity[h]])
-
-        def gate_chunk(j, carry, h=h):
-            s0 = j * chunk
-            t0 = pl.multiple_of(j * span, span)
-            tiles = [yr[halves * k + parity[h], pl.ds(t0, span), :].astype(F32) for k in range(per_half)]
-            for n in range(seqs):
-                filtered = jnp.concatenate([t[:, n * part:(n + 1) * part] for t in tiles], axis=1)
-                query = qf[pl.ds(s0, chunk), n, :, h * LANES:(h + 1) * LANES].astype(F32)
-                gated = query * filtered.reshape(chunk, rows, LANES)
-                gs[h, pl.ds(s0, chunk), n] = gated.astype(BF16)
-            return carry
-
-        lax.fori_loop(0, chunks, gate_chunk, 0)
-
-        def send_out(p, h=h):
-            pltpu.make_async_remote_copy(
-                src_ref=gs.at[h, p], dst_ref=out.at[:, :, half_cols(c, h)], send_sem=o_s, recv_sem=o_r,
-                device_id=(z, p), device_id_type=MESH).start()
-
-        each_partner(send_out)
-        pltpu.make_async_copy(gs.at[h, c], out.at[:, :, half_cols(c, h)], o_r).start()
+        for e in range(2):
+            for k in range(per_half):
+                settle(yr.at[halves * k + parity[h], e], y_r.at[halves * k + parity[h], e])
+
+            def gate_chunk(j, carry, h=h, e=e):
+                s0 = j * chunk
+                tiles = [yr[halves * k + parity[h], e, pl.ds(s0, chunk)].astype(F32).reshape(span, LANES)
+                         for k in range(per_half)]
+                for n in range(seqs):
+                    filtered = jnp.concatenate([t[:, n * part:(n + 1) * part] for t in tiles], axis=1)
+                    query = qf[e, pl.ds(s0, chunk), n, :, h * LANES:(h + 1) * LANES].astype(F32)
+                    gated = query * filtered.reshape(chunk, rows, LANES)
+                    gs[h, e, pl.ds(s0, chunk), n] = gated.astype(BF16)
+                return carry
+
+            lax.fori_loop(0, chunks // 2, gate_chunk, 0)
+
+            def send_out(p, h=h, e=e):
+                pltpu.make_async_remote_copy(
+                    src_ref=gs.at[h, e, p // 2], dst_ref=out.at[:, :, half_cols(c, h)], send_sem=o_s,
+                    recv_sem=o_r, device_id=(z, p), device_id_type=MESH).start()
+
+            for dx in around:
+                for dy in around:
+                    p = across[dx] + along[dy] + e
+                    if (dx, dy) != (0, 0):
+                        send_out(p)
+                    else:
+                        @pl.when(p != c)
+                        def _(p=p, send_out=send_out):
+                            send_out(p)
+
+                        @pl.when(p == c)
+                        def _(h=h, e=e):
+                            pltpu.make_async_copy(
+                                gs.at[h, e, c // 2], out.at[:, :, half_cols(c, h)], o_r).start()
 
     settle(kv.at[:, :, 1:nc], kv_s)
     settle(qb.at[1:nc], q_s)
-    settle(xs.at[1:nz], x_s)
+    settle(xs.at[1:nz, 0:pairs - 1, 0:LANES], x_s)
+    settle(xs.at[1:nz, pairs - 1], x_s)
     settle(ys.at[1:nz], y_s)
 
     @pl.when(z < nz - 1)
     def _():
         settle(qb.at[nc], h_s)
 
-    settle(gs.at[:, 1:nc], o_s)
+    for h in range(halves):
+        settle(gs.at[h, 0], o_s)
+        settle(gs.at[h, 1, 1:nc // 2], o_s)
     settle(out, o_r)
 
 
@@ -327,7 +362,6 @@
         by_component = jnp.transpose(proj, (0, 2, 1, 3))
         dma = pltpu.SemaphoreType.DMA
         sources = pltpu.VMEM((nz, pairs, LANES + rows, LANES), BF16)
-        results = pltpu.VMEM((nz, block, LANES), BF16)
         duo = seqs // pairs
         return pl.pallas_call(
             lambda *refs: kernel(nz, nc, *refs),
@@ -340,17 +374,18 @@
                 pltpu.VMEM(long_filter.shape, BF16),
                 pltpu.VMEM((halves, pairs, nc + 1, duo, 2, rows, LANES), BF16),
                 pltpu.VMEM((nc + 1, seqs, rows, chans), BF16),
-                pltpu.VMEM((nc, seqs, rows, chans), BF16),
+                pltpu.VMEM((2, nc // 2, seqs, rows, chans), BF16),
                 sources, sources,
                 pltpu.VMEM((nz + 1, block, LANES), BF16),
                 pltpu.VMEM((nz, rows, LANES), F32),
                 pltpu.VMEM((short_w.shape[0], 2, rows, LANES), F32),
-                results, results,
-                pltpu.VMEM((halves, nc, seqs, rows, LANES), BF16),
+                pltpu.VMEM((nz, 2, nc // 2, rows, LANES), BF16),
+                pltpu.VMEM((nz, 2, nc // 2, rows, LANES), BF16),
+                pltpu.VMEM((halves, 2, nc // 2, seqs, rows, LANES), BF16),
                 pltpu.VMEM((own, block, length), BF16),
                 pltpu.VMEM((groups, length + LANES), F32),
                 dma((3,)), dma, dma((halves, pairs)), dma, dma((2,)), dma, dma,
-                dma, dma((nz, pairs)), dma, dma((nz,)), dma, dma,
+                dma, dma((nz, pairs)), dma, dma((nz, 2)), dma, dma,
             ],
             compiler_params=pltpu.CompilerParams(collective_id=0, has_side_effects=True),
             name="hyena",

time: 51 us -> 48.3 us (0.947)
  the two profiles are of different devices: /device:TPU:66 before, /device:TPU:1 now
where the time goes in v4:
time: 48.3 us; the launch traced here: 48.2 us
  Pallas kernels  47.4 us (98%)
  local copies, waits for them, and re-layouts  0.8 us (2%)
    pallas_call x1, Pallas kernels, shards(): pl.pallas_call(lambda *refs: kernel(nz, nc, *refs), out_shape=pltpu.VMEM(...  47.4 us

profile of v4, /device:TPU:1, one launch (start us, length us, event | category | flops | bytes accessed | tf_op | source)
XLA Modules:
  0.0 48.2 jit_solution(11776109894931990610)
XLA Ops:
  0.0 47.4 %hyena.1 = bf16[4,8,8192]{2,1,0:T(8,128)(2,1)S(1)} custom-call(bf16[4,3,8,8192]{3,2,1,0:T(8,128)(2,1)} %bitcast.1, f32[3,3,256]{2,1,0:T(4,128)} %refs_1_.1, bf16[16,2048]{1,0:T(8,128)(2,1)} %refs_2_.1), custom_call_target="tpu_custom_call" | custom-call | tf_op jit(solution)/shard_map/hyena/pallas_call | solution.py:366
  47.4 0.8 %copy.5 = bf16[4,8,8192]{2,1,0:T(8,128)(2,1)} copy(bf16[4,8,8192]{2,1,0:T(8,128)(2,1)S(1)} %hyena.1) | data formatting | bytes 1048576

commit v5 on v4

--- a/solution.py
+++ b/solution.py
@@ -7,6 +7,8 @@
 
 MESH = pl.DeviceIdType.MESH
 GSIZE = 16
+PIECES = 4
+SHARES = 2
 LANES = 128
 F32 = jnp.float32
 BF16 = jnp.bfloat16
@@ -26,7 +28,8 @@
     chunk = 8
     chunks = nc // chunk
     span = chunk * rows
-    folds = block // LANES
+    folds = LANES // (duo * part)
+    high = block // folds
     fold_slots = nc // folds
     strips = fold_slots // chunk
     own_half = lax.rem(z + c, halves)
@@ -166,9 +169,9 @@
 
             lax.fori_loop(0, strips, product_strip, 0)
 
-            tall = LANES
+            tall = high
             if a == pairs - 1:
-                tall = LANES + rows
+                tall = high + rows
                 rims = []
                 for n in range(seqs):
                     head, tail = kv.at[h, n // duo, 1, n % duo], kv.at[h, n // duo, nc, n % duo]
@@ -178,7 +181,7 @@
                     rims.append(jnp.where(row < 2, pltpu.roll(tail[0].astype(F32), 2, 0), rim))
                 for k in range(per_half):
                     tile = jnp.concatenate([r[:, k * part:(k + 1) * part] for r in rims], axis=1)
-                    xs[halves * k + parity[h], a, LANES:LANES + rows, :] = tile.astype(BF16)
+                    xs[halves * k + parity[h], a, high:high + rows, :] = tile.astype(BF16)
 
             for d in (2, 1, 3, 0):
                 p = halves * lax.rem(z // halves + d, per_half) + parity[h]
@@ -193,7 +196,7 @@
                 else:
                     pl.when(own_half != h)(send_x)
 
-            if (h, a) == (halves - 1, 0):
+            if (h, a) == (halves - 1, (pairs - 1) // 2):
                 each_partner(send_q)
 
             @pl.when(own_half == h)
@@ -214,14 +217,14 @@
 
     for s in range(nz):
         for a in range(pairs):
-            settle(xr.at[s, a, 0:LANES + rows * (a // (pairs - 1))], x_r.at[s, a])
+            settle(xr.at[s, a, 0:high + rows * (a // (pairs - 1))], x_r.at[s, a])
     for s in range(nz):
-        tiles = [xr[s, a, :LANES, :] for a in range(pairs)]
+        tiles = [xr[s, a, :high, :] for a in range(pairs)]
         for f in range(folds):
             at = f * LANES // folds
-            xu[nz - 1 - s, f * LANES:(f + 1) * LANES, :] = jnp.concatenate(
+            xu[nz - 1 - s, f * high:(f + 1) * high, :] = jnp.concatenate(
                 [t[:, at:at + LANES // folds] for t in tiles], axis=1)
-        edge[s] = xr[s, pairs - 1, LANES:LANES + rows, :].astype(F32)
+        edge[s] = xr[s, pairs - 1, high:high + rows, :].astype(F32)
 
     firsts, seconds = [], []
     for i in range(2):
@@ -261,17 +264,18 @@
             total = term if total is None else total + term
         for i in range(2):
             result = total[:, i * LANES:(i + 1) * LANES].astype(BF16)
-            result = result.reshape(nc // 2, 2, rows, LANES)
-            for e in range(2):
+            result = result.reshape(nc // SHARES, SHARES, rows, LANES)
+            for e in range(SHARES):
                 ys[2 * m + i, e] = result[:, e]
         if m == nz // 2 - 1:
             pl.when(own_half == 0)(pass_query_rim)
         if m % 2 == 1:
             for p in range(2 * m - 2, 2 * m + 2):
                 send_y(p, 0)
-    for p in range(nz):
-        send_y(p, 1)
-    for e in range(2):
+    for e in range(1, SHARES):
+        for p in range(nz):
+            send_y(p, e)
+    for e in range(SHARES):
         pltpu.make_async_copy(ys.at[z, e], yr.at[z, e], y_r.at[z, e]).start()
 
     settle(qb.at[1:nc], q_r.at[0])
@@ -286,15 +290,16 @@
             for n in range(seqs):
                 ext = qb[pl.ds(s0, chunk + 1), n, :, h * LANES:(h + 1) * LANES].astype(F32)
                 value = feature(ext.reshape((chunk + 1) * rows, LANES), 0, h)
-                value = value.astype(BF16).reshape(chunk // 2, 2, rows, LANES)
-                for e in range(2):
-                    qf[e, pl.ds(j * (chunk // 2), chunk // 2), n, :, h * LANES:(h + 1) * LANES] = value[:, e]
+                few = chunk // SHARES
+                value = value.astype(BF16).reshape(few, SHARES, rows, LANES)
+                for e in range(SHARES):
+                    qf[e, pl.ds(j * few, few), n, :, h * LANES:(h + 1) * LANES] = value[:, e]
         return carry
 
     lax.fori_loop(0, chunks, query_chunk, 0)
 
     for h in range(halves):
-        for e in range(2):
+        for e in range(SHARES):
             for k in range(per_half):
                 settle(yr.at[halves * k + parity[h], e], y_r.at[halves * k + parity[h], e])
 
@@ -309,11 +314,11 @@
                     gs[h, e, pl.ds(s0, chunk), n] = gated.astype(BF16)
                 return carry
 
-            lax.fori_loop(0, chunks // 2, gate_chunk, 0)
+            lax.fori_loop(0, chunks // SHARES, gate_chunk, 0)
 
             def send_out(p, h=h, e=e):
                 pltpu.make_async_remote_copy(
-                    src_ref=gs.at[h, e, p // 2], dst_ref=out.at[:, :, half_cols(c, h)], send_sem=o_s,
+                    src_ref=gs.at[h, e, p // SHARES], dst_ref=out.at[:, :, half_cols(c, h)], send_sem=o_s,
                     recv_sem=o_r, device_id=(z, p), device_id_type=MESH).start()
 
             for dx in around:
@@ -329,11 +334,11 @@
                         @pl.when(p == c)
                         def _(h=h, e=e):
                             pltpu.make_async_copy(
-                                gs.at[h, e, c // 2], out.at[:, :, half_cols(c, h)], o_r).start()
+                                gs.at[h, e, c // SHARES], out.at[:, :, half_cols(c, h)], o_r).start()
 
     settle(kv.at[:, :, 1:nc], kv_s)
     settle(qb.at[1:nc], q_s)
-    settle(xs.at[1:nz, 0:pairs - 1, 0:LANES], x_s)
+    settle(xs.at[1:nz, 0:pairs - 1, 0:high], x_s)
     settle(xs.at[1:nz, pairs - 1], x_s)
     settle(ys.at[1:nz], y_s)
 
@@ -341,9 +346,8 @@
     def _():
         settle(qb.at[nc], h_s)
 
-    for h in range(halves):
-        settle(gs.at[h, 0], o_s)
-        settle(gs.at[h, 1, 1:nc // 2], o_s)
+    settle(gs.at[:, 0:SHARES - 1], o_s)
+    settle(gs.at[:, SHARES - 1, 1:nc // SHARES], o_s)
     settle(out, o_r)
 
 
@@ -356,13 +360,13 @@
         block = rows * nc
         halves = chans // LANES
         part = chans // nz
-        pairs = seqs * part // LANES * (block // LANES)
+        pairs = PIECES
         groups, length = long_filter.shape
         own = part // GSIZE
         by_component = jnp.transpose(proj, (0, 2, 1, 3))
         dma = pltpu.SemaphoreType.DMA
-        sources = pltpu.VMEM((nz, pairs, LANES + rows, LANES), BF16)
-        duo = seqs // pairs
+        duo = seqs // PIECES
+        sources = pltpu.VMEM((nz, PIECES, block * duo * part // LANES + rows, LANES), BF16)
         return pl.pallas_call(
             lambda *refs: kernel(nz, nc, *refs),
             out_shape=pltpu.VMEM((seqs, rows, width), BF16),
@@ -374,18 +378,18 @@
                 pltpu.VMEM(long_filter.shape, BF16),
                 pltpu.VMEM((halves, pairs, nc + 1, duo, 2, rows, LANES), BF16),
                 pltpu.VMEM((nc + 1, seqs, rows, chans), BF16),
-                pltpu.VMEM((2, nc // 2, seqs, rows, chans), BF16),
+                pltpu.VMEM((SHARES, nc // SHARES, seqs, rows, chans), BF16),
                 sources, sources,
                 pltpu.VMEM((nz + 1, block, LANES), BF16),
                 pltpu.VMEM((nz, rows, LANES), F32),
                 pltpu.VMEM((short_w.shape[0], 2, rows, LANES), F32),
-                pltpu.VMEM((nz, 2, nc // 2, rows, LANES), BF16),
-                pltpu.VMEM((nz, 2, nc // 2, rows, LANES), BF16),
-                pltpu.VMEM((halves, 2, nc // 2, seqs, rows, LANES), BF16),
+                pltpu.VMEM((nz, SHARES, nc // SHARES, rows, LANES), BF16),
+                pltpu.VMEM((nz, SHARES, nc // SHARES, rows, LANES), BF16),
+                pltpu.VMEM((halves, SHARES, nc // SHARES, seqs, rows, LANES), BF16),
                 pltpu.VMEM((own, block, length), BF16),
                 pltpu.VMEM((groups, length + LANES), F32),
                 dma((3,)), dma, dma((halves, pairs)), dma, dma((2,)), dma, dma,
-                dma, dma((nz, pairs)), dma, dma((nz, 2)), dma, dma,
+                dma, dma((nz, pairs)), dma, dma((nz, SHARES)), dma, dma,
             ],
             compiler_params=pltpu.CompilerParams(collective_id=0, has_side_effects=True),
             name="hyena",

time: 48.3 us -> 48 us (level)
  no operation moved by 1% of the time
where the time goes in v5:
time: 48 us; the launch traced here: 47.9 us
  Pallas kernels  47.1 us (98%)
  local copies, waits for them, and re-layouts  0.8 us (2%)
    pallas_call x1, Pallas kernels, shards(): pl.pallas_call(lambda *refs: kernel(nz, nc, *refs), out_shape=pltpu.VMEM(...  47.1 us

profile of v5, /device:TPU:1, one launch (start us, length us, event | category | flops | bytes accessed | tf_op | source)
XLA Modules:
  0.0 47.9 jit_solution(2551958069900860400)
XLA Ops:
  0.0 47.1 %hyena.1 = bf16[4,8,8192]{2,1,0:T(8,128)(2,1)S(1)} custom-call(bf16[4,3,8,8192]{3,2,1,0:T(8,128)(2,1)} %bitcast.1, f32[3,3,256]{2,1,0:T(4,128)} %refs_1_.1, bf16[16,2048]{1,0:T(8,128)(2,1)} %refs_2_.1), custom_call_target="tpu_custom_call" | custom-call | tf_op jit(solution)/shard_map/hyena/pallas_call | solution.py:370
  47.1 0.8 %copy.5 = bf16[4,8,8192]{2,1,0:T(8,128)(2,1)} copy(bf16[4,8,8192]{2,1,0:T(8,128)(2,1)S(1)} %hyena.1) | data formatting | bytes 1048576

commit v6 on v5

--- a/solution.py
+++ b/solution.py
@@ -63,25 +63,22 @@
     def greet(p):
         pl.semaphore_signal(barrier, inc=1, device_id=(z, p), device_id_type=MESH)
 
-    for n in range(seqs):
-        pltpu.make_async_copy(proj_in.at[n], proj.at[n], in_r.at[0]).start()
-    pltpu.make_async_copy(lf_in, lf_ref, in_r.at[1]).start()
-    pltpu.make_async_copy(w_in, w_ref, in_r.at[2]).start()
     each_partner(greet)
     for d in line:
         pl.semaphore_signal(barrier, inc=1, device_id=(lax.rem(z + d, nz), c), device_id_type=MESH)
-    settle(proj, in_r.at[0])
+    for n in range(seqs):
+        pltpu.make_async_copy(proj_in.at[n], proj.at[n], in_r.at[n]).start()
+    pltpu.make_async_copy(lf_in, lf_ref, in_r.at[seqs]).start()
+    pltpu.make_async_copy(w_in, w_ref, in_r.at[seqs + 1]).start()
     last = c // (nc - 1)
+    pl.semaphore_wait(barrier, nc - 1 + nz - 1)
+
     for h in range(halves):
         for a in range(pairs):
-            pltpu.make_async_copy(
-                proj.at[a * duo:(a + 1) * duo, 1:3, :, half_cols(c, h)], kv.at[h, a, c + 1],
-                kv_r.at[h, a]).start()
-    pltpu.make_async_copy(proj.at[:, 0, :, cols(c)], qb.at[c + 1], q_r.at[last]).start()
-    pl.semaphore_wait(barrier, nc - 1 + nz - 1)
-
-    for h in range(halves):
-        for a in range(pairs):
+            if h == 0:
+                for n in range(a * duo, (a + 1) * duo):
+                    settle(proj.at[n], in_r.at[n])
+
             def send_kv(p, h=h, a=a):
                 pltpu.make_async_remote_copy(
                     src_ref=proj.at[a * duo:(a + 1) * duo, 1:3, :, half_cols(p, h)],
@@ -89,9 +86,13 @@
                     device_id=(z, p), device_id_type=MESH).start()
 
             each_partner(send_kv)
-
-    settle(lf_ref, in_r.at[1])
-    settle(w_ref, in_r.at[2])
+            pltpu.make_async_copy(
+                proj.at[a * duo:(a + 1) * duo, 1:3, :, half_cols(c, h)], kv.at[h, a, c + 1],
+                kv_r.at[h, a]).start()
+    pltpu.make_async_copy(proj.at[:, 0, :, cols(c)], qb.at[c + 1], q_r.at[last]).start()
+
+    settle(lf_ref, in_r.at[seqs])
+    settle(w_ref, in_r.at[seqs + 1])
 
     length = lf_ref.shape[1]
     pieces = length // LANES
@@ -245,13 +246,6 @@
 
     lane = lax.broadcasted_iota(jnp.int32, (1, 2 * LANES), 1)
 
-    def send_y(p, e):
-        @pl.when(z != p)
-        def _():
-            pltpu.make_async_remote_copy(
-                src_ref=ys.at[p, e], dst_ref=yr.at[z, e], send_sem=y_s, recv_sem=y_r.at[z, e],
-                device_id=(p, c), device_id_type=MESH).start()
-
     for m in range(nz // 2):
         lags = 2 * m + 2
         even = xu[nz - 1 - 2 * m:nz - 1 - 2 * m + lags].reshape(lags * block, LANES)
@@ -267,15 +261,16 @@
             result = result.reshape(nc // SHARES, SHARES, rows, LANES)
             for e in range(SHARES):
                 ys[2 * m + i, e] = result[:, e]
-        if m == nz // 2 - 1:
+    for e in range(SHARES):
+        for p in (0, 4, 1, 5, 2, 6, 3, 7):
+            @pl.when(z != p)
+            def _(p=p, e=e):
+                pltpu.make_async_remote_copy(
+                    src_ref=ys.at[p, e], dst_ref=yr.at[z, e], send_sem=y_s, recv_sem=y_r.at[z, e],
+                    device_id=(p, c), device_id_type=MESH).start()
+
+        if e == 0:
             pl.when(own_half == 0)(pass_query_rim)
-        if m % 2 == 1:
-            for p in range(2 * m - 2, 2 * m + 2):
-                send_y(p, 0)
-    for e in range(1, SHARES):
-        for p in range(nz):
-            send_y(p, e)
-    for e in range(SHARES):
         pltpu.make_async_copy(ys.at[z, e], yr.at[z, e], y_r.at[z, e]).start()
 
     settle(qb.at[1:nc], q_r.at[0])
@@ -388,7 +383,7 @@
                 pltpu.VMEM((halves, SHARES, nc // SHARES, seqs, rows, LANES), BF16),
                 pltpu.VMEM((own, block, length), BF16),
                 pltpu.VMEM((groups, length + LANES), F32),
-                dma((3,)), dma, dma((halves, pairs)), dma, dma((2,)), dma, dma,
+                dma((seqs + 2,)), dma, dma((halves, pairs)), dma, dma((2,)), dma, dma,
                 dma, dma((nz, pairs)), dma, dma((nz, SHARES)), dma, dma,
             ],
             compiler_params=pltpu.CompilerParams(collective_id=0, has_side_effects=True),

time: 48 us -> 47.6 us (level)
  no operation moved by 1% of the time
where the time goes in v6:
time: 47.6 us; the launch traced here: 47.5 us
  Pallas kernels  46.7 us (98%)
  local copies, waits for them, and re-layouts  0.8 us (2%)
    pallas_call x1, Pallas kernels, shards(): pl.pallas_call(lambda *refs: kernel(nz, nc, *refs), out_shape=pltpu.VMEM(...  46.7 us

profile of v6, /device:TPU:1, one launch (start us, length us, event | category | flops | bytes accessed | tf_op | source)
XLA Modules:
  0.0 47.5 jit_solution(15462904157349968602)
XLA Ops:
  0.0 46.7 %hyena.1 = bf16[4,8,8192]{2,1,0:T(8,128)(2,1)S(1)} custom-call(bf16[4,3,8,8192]{3,2,1,0:T(8,128)(2,1)} %bitcast.1, f32[3,3,256]{2,1,0:T(4,128)} %refs_1_.1, bf16[16,2048]{1,0:T(8,128)(2,1)} %refs_2_.1), custom_call_target="tpu_custom_call" | custom-call | tf_op jit(solution)/shard_map/hyena/pallas_call | solution.py:365
  46.7 0.8 %copy.5 = bf16[4,8,8192]{2,1,0:T(8,128)(2,1)} copy(bf16[4,8,8192]{2,1,0:T(8,128)(2,1)S(1)} %hyena.1) | data formatting | bytes 1048576
